TPU v7x, 32 devices: a whole 2x2x4 slice. The times are simulated.
32 devices in a mesh: rep: 2 (over y), dp: 4 (over x, core), tensor: 4 (over z).
Axes of the slice: x: 2, y: 2, z: 4, core: 2. Of those that a mesh axis runs over, the one named last changes fastest.
Arguments:
- activations: bfloat16 [12288, 8192], P(('rep', 'dp'), 'tensor'), parts along dimension 0, may hold values from -6 to 6
- output_gradient: bfloat16 [12288, 2048], P(('rep', 'dp'), 'tensor'), parts along dimension 0, may hold values from -6 to 6
- row_tenant: int32 [12288, 1], P(('rep', 'dp')), parts along dimension 0, may hold values from 0 to 15; in each aligned block of 1536 rows (0 to 1535, 1536 to 3071, ...) at most 192 rows name the same one
- group_row_count: int32 [8], P(('rep', 'dp')), parts along dimension 0, may hold values from 384 to 1536
- tenant_storage_entry: int32 [16], replicated, may hold values from 0 to 15, each once
- key_value_weight: bfloat16 [8192, 2048], P('tensor'), may hold values from -0.125 to 0.125
- adapter_down_maps: bfloat16 [16, 8192, 64], P('dp', 'tensor'), may hold values from -0.23925781 to 0.23925781
- adapter_up_maps: bfloat16 [16, 64, 2048], P('dp', None, 'tensor'), may hold values from -0.125 to 0.125
- down_row_factor: float32 [16, 8192], P('dp', 'tensor'), may hold values from 2 to 60
- down_column_factor: float32 [16, 64], P('dp'), may hold values from 2 to 60
- up_row_factor: float32 [16, 64], P('dp'), may hold values from 0.02 to 0.6
- up_column_factor: float32 [16, 2048], P('dp', 'tensor'), may hold values from 20 to 600
Outputs:
- input_grad: bfloat16 [12288, 8192], P(('rep', 'dp'), 'tensor'), parts along dimension 0
- down_rows: float32 [32, 8192], P(('rep', 'dp'), 'tensor'), parts along dimension 0
- down_cols: float32 [32, 64], P(('rep', 'dp')), parts along dimension 0
- up_rows: float32 [32, 64], P(('rep', 'dp')), parts along dimension 0
- up_cols: float32 [32, 2048], P(('rep', 'dp'), 'tensor'), parts along dimension 0
- down_update: float32 [32, 8192, 64], P(('rep', 'dp'), 'tensor'), parts along dimension 0
- up_update: float32 [32, 64, 2048], P(('rep', 'dp'), None, 'tensor'), parts along dimension 0
There are 2 independent parts, one for each index of `rep`. A program takes and returns all parts, laid end to end along the dimension named above; an argument that names none is the same for every part. Nothing has to cross between parts.
Inputs may be any that keep to these rules, and one draw needn't show every extreme that they name: `row_tenant`: within the rows of one group (aligned blocks of 1536 rows, padding rows included) no tenant is named by more than 192 rows, a bound that some block reaches. Row 1536 g + i is live for i < group_row_count[g]; the other rows of the group are padding. A permutation: tenant t's adapters and factors are stored at entry tenant_storage_entry[t] of the adapter and factor arrays.
All inputs are finite; a program needn't handle non-finite values.
Results may differ from a plain program's by a relative error of at most 0.0029.
Values may be sent and summed in bfloat16 or wider, within the bound.
No kernel may reach another device: no remote copies, remote signals or barrier semaphores. Data moves between devices by JAX's collectives and lax.ppermute only.
A program may use at most 128 MiB of HBM per device.

v0:
```python
import jax
import jax.numpy as jnp
from jax import lax
from jax.sharding import PartitionSpec as P

adapter_scale = 0.25
decay_rate = 0.9
tiny_floor = 1e-30


def slot_layout(tenant_col, tenant_storage_entry, row_limit):
    tenants = tenant_col[:, 0]
    count_rows = tenants.shape[0]
    entries = tenant_storage_entry.shape[0]
    onehot = (tenants[:, None] == jnp.arange(entries, dtype=jnp.int32)[None, :]).astype(jnp.int32)
    position = jnp.cumsum(onehot, axis=0) - onehot
    within = jnp.sum(position * onehot, axis=1)
    entry_of = jnp.sum(onehot * tenant_storage_entry[None, :], axis=1)
    target = entry_of * row_limit + within
    lookup = (
        jnp.full((entries * row_limit,), count_rows, jnp.int32)
        .at[target]
        .set(jnp.arange(count_rows, dtype=jnp.int32))
    )
    return (target, lookup)


def shards(
    activations,
    output_gradient,
    row_tenant,
    group_row_count,
    tenant_storage_entry,
    key_value_weight,
    adapter_down_maps,
    adapter_up_maps,
    down_row_factor,
    down_column_factor,
    up_row_factor,
    up_column_factor,
):
    group_total = lax.axis_size("dp")
    owned_row_count = adapter_down_maps.shape[0]
    entries = owned_row_count * group_total
    count_rows = activations.shape[0]
    row_limit = 2 * count_rows // entries
    full_width = key_value_weight.shape[0] * lax.axis_size("tensor")
    pair_width = key_value_weight.shape[1]
    live_mask = jnp.arange(count_rows, dtype=jnp.int32)[:, None] < group_row_count[0]
    masked = jnp.where(live_mask, output_gradient, jnp.zeros_like(output_gradient))
    frozen = lax.dot_general(
        lax.all_gather(masked, "tensor", axis=1, tiled=True),
        key_value_weight,
        (((1,), (1,)), ((), ())),
        preferred_element_type=jnp.float32,
    )
    target, lookup = slot_layout(row_tenant, tenant_storage_entry, row_limit)
    padded_x = jnp.concatenate(
        [activations, jnp.zeros((1, activations.shape[1]), activations.dtype)], axis=0
    )
    padded_g = jnp.concatenate([masked, jnp.zeros((1, masked.shape[1]), masked.dtype)], axis=0)
    storage_input = padded_x[lookup]
    slot_g = padded_g[lookup]
    every_down, every_up = (
        lax.all_gather(adapter_down_maps, "dp", axis=0, tiled=True),
        lax.all_gather(adapter_up_maps, "dp", axis=0, tiled=True),
    )
    group_x = storage_input.reshape(entries, row_limit, storage_input.shape[1])
    group_g = slot_g.reshape(entries, row_limit, slot_g.shape[1])
    partial_down = jnp.einsum(
        "tcd,tdr->tcr", group_x, every_down, preferred_element_type=jnp.float32
    )
    partial_up = jnp.einsum("tck,trk->tcr", group_g, every_up, preferred_element_type=jnp.float32)
    proj_down, proj_up = lax.psum((partial_down, partial_up), "tensor")
    rounded_down = proj_down.astype(jnp.bfloat16)
    rounded_up = proj_up.astype(jnp.bfloat16)
    term_down = adapter_scale * jnp.einsum(
        "tcd,tcr->tdr", group_x, rounded_up, preferred_element_type=jnp.float32
    )
    term_up = adapter_scale * jnp.einsum(
        "tcr,tck->trk", rounded_down, group_g, preferred_element_type=jnp.float32
    )
    down_gradient, up_gradient = (
        lax.psum_scatter(term_down, "dp", scatter_dimension=0, tiled=True),
        lax.psum_scatter(term_up, "dp", scatter_dimension=0, tiled=True),
    )
    adapter_branch = (
        adapter_scale
        * jnp.einsum("tcr,tdr->tcd", rounded_up, every_down, preferred_element_type=jnp.float32)
    ).astype(jnp.bfloat16)
    side_slots = adapter_branch.reshape(entries * row_limit, storage_input.shape[1])
    side_rows = side_slots[target]
    input_grad = (frozen + side_rows.astype(jnp.float32)).astype(jnp.bfloat16)
    square_down = down_gradient * down_gradient + tiny_floor
    square_up = up_gradient * up_gradient + tiny_floor
    down_rows = decay_rate * down_row_factor + (1.0 - decay_rate) * jnp.mean(square_down, axis=2)
    up_cols = decay_rate * up_column_factor + (1.0 - decay_rate) * jnp.mean(square_up, axis=1)
    column_total, row_total, rows_sum = lax.psum(
        (jnp.sum(square_down, axis=1), jnp.sum(square_up, axis=2), jnp.sum(down_rows, axis=1)),
        "tensor",
    )
    down_cols = decay_rate * down_column_factor + (1.0 - decay_rate) * (column_total / full_width)
    up_rows = decay_rate * up_row_factor + (1.0 - decay_rate) * (row_total / pair_width)
    second_down = (
        down_rows[:, :, None] * down_cols[:, None, :] / (rows_sum / full_width)[:, None, None]
    )
    second_up = up_rows[:, :, None] * up_cols[:, None, :] / jnp.mean(up_rows, axis=1)[:, None, None]
    down_update = down_gradient * lax.rsqrt(second_down)
    up_update = up_gradient * lax.rsqrt(second_up)
    return (input_grad, down_rows, down_cols, up_rows, up_cols, down_update, up_update)


def solution(mesh):
    in_specs = (
        P(("rep", "dp"), "tensor"),
        P(("rep", "dp"), "tensor"),
        P(("rep", "dp"), None),
        P(("rep", "dp")),
        P(),
        P("tensor", None),
        P("dp", "tensor", None),
        P("dp", None, "tensor"),
        P("dp", "tensor"),
        P("dp", None),
        P("dp", None),
        P("dp", "tensor"),
    )
    out_specs = (
        P(("rep", "dp"), "tensor"),
        P(("rep", "dp"), "tensor"),
        P(("rep", "dp"), None),
        P(("rep", "dp"), None),
        P(("rep", "dp"), "tensor"),
        P(("rep", "dp"), "tensor", None),
        P(("rep", "dp"), None, "tensor"),
    )
    return jax.shard_map(shards, mesh=mesh, in_specs=in_specs, out_specs=out_specs, check_vma=False)
```

profile of v0, /device:TPU:0, one launch (start us, length us, event | category | flops | bytes accessed | tf_op | source)
XLA Modules:
  0.0 379.9 jit_solution(5909354718288648986)
XLA Ops:
  7.2 0.7 all-gather.6.cloned.1.call-update
  8.0 0.7 all-gather.8.cloned.1.call-update
  9.4 2.8 broadcast_select_fusion
  12.3 4.6 %reduce-window.6 = s32[16,12,128]{2,1,0:T(8,128)S(1)} reduce-window(s32[16,12,128]{2,1,0:T(8,128)S(1)} %fusion.7, s32[]{:T(128)} %constant.17.clone.1), window={size=1x1x128 pad=0_0x0_0x127_0}, to_apply=%region_1.2 | reduce-window | flops 3121152 | bytes 196612 | tf_op jit(solution)/shard_map/reduce-window
  17.5 1.6 concatenate.6
  19.1 6.7 %concatenate.7 = bf16[1537,2048]{1,0:T(8,128)(2,1)} pad(bf16[1536,2048]{1,0:T(8,128)(2,1)} %param.12, bf16[]{:T(256)} %constant.15.clone.1), padding=0_1x0_0 | pad | bytes 12587010 | tf_op jit(solution)/shard_map/concatenate | solution.py:58
  26.0 6.2 %scatter_custom_fusion = s32[3072]{0:T(1024)S(1)} fusion(s32[1536]{0:T(1024)S(1)} %fusion.12, s32[1536]{0:T(1024)S(1)} %iota.17, s32[]{:T(128)} %constant.16.clone.1), kind=kCustom, calls=%fused_computation.39 | custom fusion | bytes 12292 | tf_op jit(solution)/shard_map/scatter | solution.py:23
  32.2 27.4 %gather_fusion.2 = bf16[3072,2048]{1,0:T(8,128)(2,1)} fusion(bf16[1537,2048]{1,0:T(8,128)(2,1)} %concatenate.7, s32[3072]{0:T(1024)S(1)} %fusion.11), kind=kCustom, calls=%fused_computation.2 | custom fusion | bytes 25178112 | tf_op jit(solution)/shard_map/gather | solution.py:62
  59.7 13.3 %gather_fusion = bf16[3072,512]{1,0:T(8,128)(2,1)} fusion(bf16[1537,512]{1,0:T(8,128)(2,1)S(1)} %concatenate.6, s32[3072]{0:T(1024)S(1)} %fusion.11), kind=kCustom, calls=%fused_computation | custom fusion | bytes 6303744 | tf_op jit(solution)/shard_map/gather | solution.py:63
  72.9 4.8 %fusion.17 = f32[16,192,64]{1,2,0:T(8,128)} fusion(bf16[16,192,512]{2,1,0:T(8,128)(2,1)} %bitcast.39, bf16[16,64,512]{2,1,0:T(8,128)(2,1)} %all-gather.6.cloned.1.call-done), kind=kOutput, calls=%fused_computation.47 | convolution fusion | flops 201326592 | bytes 4980736 | tf_op jit(solution)/shard_map/tck,trk->tcr/dot_general | solution.py:73
  77.7 11.1 %fusion.18 = f32[16,192,64]{1,2,0:T(8,128)} fusion(bf16[16,192,2048]{2,1,0:T(8,128)(2,1)} %bitcast.37, bf16[16,2048,64]{1,2,0:T(8,128)(2,1)} %all-gather.8.cloned.1.call-done), kind=kOutput, calls=%fused_computation.48 | convolution fusion | flops 805306368 | bytes 17563648 | tf_op jit(solution)/shard_map/tcd,tdr->tcr/dot_general | solution.py:70
  88.9 153.0 %all-reduce.5 = (bf16[16,192,64]{1,2,0:T(8,128)(2,1)}, bf16[16,192,64]{1,2,0:T(8,128)(2,1)}) all-reduce(f32[16,192,64]{1,2,0:T(8,128)} %fusion.17, f32[16,192,64]{1,2,0:T(8,128)} %fusion.18), channel_id=1, replica_groups=mesh['rep'=2,'dp'=4,'tensor'=4] {'tensor'}, use_global_device_ids=true, to_apply=%region_5.6 | all-reduce | flops 393216 | bytes 2359296 | tf_op jit(solution)/shard_map/psum | solution.py:74
  241.8 3.1 convolution_multiply_fusion.1
  245.2 10.5 %convolution_multiply_fusion = f32[16,2048,64]{1,2,0:T(8,128)} fusion(bf16[16,192,2048]{2,1,0:T(8,128)(2,1)} %bitcast.38, bf16[16,192,64]{1,2,0:T(8,128)(2,1)} %get-tuple-element.16), kind=kOutput, calls=%fused_computation.6 | convolution fusion | flops 807403520 | bytes 21364736 | tf_op jit(solution)/shard_map/tcd,tcr->tdr/dot_general | solution.py:77
  255.7 1.0 copy-done.2
  256.7 10.7 %multiply_convert_fusion = bf16[16,192,2048]{2,1,0:T(8,128)(2,1)} fusion(bf16[16,2048,64]{1,2,0:T(8,128)(2,1)} %all-gather.8.cloned.1.call-done, bf16[16,192,64]{1,2,0:T(8,128)(2,1)S(1)} %copy-done.2), kind=kOutput, calls=%fused_computation.4 | convolution fusion | flops 817889280 | bytes 17170432 | tf_op jit(solution)/shard_map/tcr,tdr->tcd/dot_general | solution.py:89
  267.3 19.1 %gather_fusion.1 = bf16[1536,2048]{1,0:T(8,128)(2,1)} fusion(bf16[3072,2048]{1,0:T(8,128)(2,1)} %bitcast.36, s32[2048]{0:T(1024)S(1)} %pad_clamp_fusion), kind=kCustom, calls=%fused_computation.1 | custom fusion | bytes 12589056 | tf_op jit(solution)/shard_map/gather | solution.py:92
  286.5 21.2 %add_convert_fusion = bf16[1536,2048]{1,0:T(8,128)(2,1)} fusion(bf16[1536,2048]{1,0:T(8,128)(2,1)} %gather_fusion.1, bf16[1536,2048]{1,0:T(8,128)(2,1)} %all-gather.4.cloned.1.call-done, bf16[2048,2048]{1,0:T(8,128)(2,1)} %param.17), kind=kOutput, calls=%fused_computation.5 | convolution fusion | flops 12894339072 | bytes 27262976 | tf_op jit(solution)/shard_map/dot_general | solution.py:51
  307.7 1.2 fusion.3
  308.9 46.4 %reduce-scatter.3.cloned.1.call-done = f32[4,2048,64]{1,2,0:T(8,128)} async-done(((f32[16,2048,64]{1,2,0:T(8,128)}), f32[4,2048,64]{1,2,0:T(8,128)}) %reduce-scatter.3.cloned.1.call-update) | async-done | bytes 2097168 | tf_op jit(solution)/shard_map/reduce_scatter | solution.py:84
  355.3 2.2 fusion
  357.6 11.9 %all-reduce.2 = (f32[4,64]{1,0:T(4,128)S(1)}, f32[4,64]{1,0:T(4,128)S(1)}, f32[4]{0:T(128)S(1)}) all-reduce(f32[4,64]{1,0:T(4,128)S(1)} %get-tuple-element.7, f32[4,64]{1,0:T(4,128)S(1)} %get-tuple-element.10, f32[4]{0:T(128)S(1)} %get-tuple-element.20), channel_id=1, replica_groups=mesh['rep'=2,'dp'=4,'tensor'=4] {'tensor'}, use_global_device_ids=true, to_apply=%region_9.10 | all-reduce | flops 516 | bytes 4128 | tf_op jit(solution)/shard_map/psum | solution.py:98
  369.7 2.0 rsqrt_multiply_fusion.1
  371.7 1.7 rsqrt_multiply_fusion
  (54 shorter events, 1.6 us)
Async XLA Ops:
  7.2 5.1 %copy-start.9 = (s32[1536,1]{0,1:T(1,128)S(1)}, s32[1536,1]{0,1:T(1,128)}, u32[]{:S(2)}) copy-start(s32[1536,1]{0,1:T(1,128)} %param.14) | copy-start | bytes 18436
  7.2 65.8 %all-gather.6.cloned.1.call-start = ((), (), s32[]{:S(2)}) async-start(), calls=%async_computation.3 | async-start | bytes 1310720 | tf_op jit(solution)/shard_map/all_gather | solution.py:66
  7.9 69.8 %all-gather.8.cloned.1.call-start = ((), (), s32[]{:S(2)}) async-start(), calls=%async_computation.4 | async-start | bytes 5242880 | tf_op jit(solution)/shard_map/all_gather | solution.py:65
  8.7 277.8 %all-gather.4.cloned.1.call-start = ((), (), s32[]{:S(2)}) async-start(), calls=%async_computation.2 | async-start | bytes 7864320 | tf_op jit(solution)/shard_map/all_gather | solution.py:52
  12.2 295.5 %reduce-scatter.5.cloned.1.call-start = ((), (), s32[]{:S(2)}) async-start(), calls=%async_computation.6 | async-start | bytes 2621440 | tf_op jit(solution)/shard_map/reduce_scatter | solution.py:85
  19.0 6.8 %copy-start.12 = (s32[16]{0:T(128)S(1)}, s32[16]{0:T(128)}, u32[]{:S(2)}) copy-start(s32[16]{0:T(128)} %param.16) | copy-start | bytes 196
  77.7 164.1 %copy-start = (bf16[3072,512]{1,0:T(8,128)(2,1)S(1)}, bf16[3072,512]{1,0:T(8,128)(2,1)}, u32[]{:S(2)}) copy-start(bf16[3072,512]{1,0:T(8,128)(2,1)} %gather_fusion) | copy-start | bytes 9437188
  244.9 110.3 %reduce-scatter.3.cloned.1.call-start = ((), (), s32[]{:S(2)}) async-start(), calls=%async_computation.5 | async-start | bytes 10485760 | tf_op jit(solution)/shard_map/reduce_scatter | solution.py:84
  255.6 1.0 copy-start.2
  286.4 22.4 %copy-start.8 = (f32[4,512]{1,0:T(4,128)S(1)}, f32[4,512]{1,0:T(4,128)}, u32[]{:S(2)}) copy-start(f32[4,512]{1,0:T(4,128)} %param.23) | copy-start | bytes 24580
  286.4 71.0 %copy-start.5 = (f32[4,2048]{1,0:T(4,128)S(1)}, f32[4,2048]{1,0:T(4,128)}, u32[]{:S(2)}) copy-start(f32[4,2048]{1,0:T(4,128)} %param.20) | copy-start | bytes 98308
  286.4 83.1 %copy-start.10 = (f32[4,64]{1,0:T(4,128)S(1)}, f32[4,64]{1,0:T(4,128)}, u32[]{:S(2)}) copy-start(f32[4,64]{1,0:T(4,128)} %param.22) | copy-start | bytes 3076
  286.4 83.1 %copy-start.11 = (f32[4,64]{1,0:T(4,128)S(1)}, f32[4,64]{1,0:T(4,128)}, u32[]{:S(2)}) copy-start(f32[4,64]{1,0:T(4,128)} %param.21) | copy-start | bytes 3076
  308.9 64.4 %copy-start.4 = (f32[4,512]{1,0:T(4,128)}, f32[4,512]{1,0:T(4,128)S(1)}, u32[]{:S(2)}) copy-start(f32[4,512]{1,0:T(4,128)S(1)} %multiply_add_fusion.3) | copy-start | bytes 24580
  355.3 16.4 %copy-start.1 = (f32[4,2048,64]{1,2,0:T(8,128)S(1)}, f32[4,2048,64]{1,2,0:T(8,128)}, u32[]{:S(2)}) copy-start(f32[4,2048,64]{1,2,0:T(8,128)} %reduce-scatter.3.cloned.1.call-done) | copy-start | bytes 6291460
  357.6 15.8 %copy-start.3 = (f32[4,2048]{1,0:T(4,128)}, f32[4,2048]{1,0:T(4,128)S(1)}, u32[]{:S(2)}) copy-start(f32[4,2048]{1,0:T(4,128)S(1)} %get-tuple-element.21) | copy-start | bytes 98308
  369.6 3.7 copy-start.6
  369.6 3.7 copy-start.7
Sparse Core Ops, SparseCore 0:
  9.5 19.4 all-gather.5
  30.6 34.4 all-gather.7
  66.6 182.3 all-gather.3
  252.0 29.3 reduce-scatter.4
  283.8 71.4 reduce-scatter.2
where the time goes:
time: 380 us
  blocking collectives  165 us (43%)
  local copies, waits for them, and re-layouts  75.8 us (20%)
  matrix products  61.3 us (16%)
  waiting for transfers between devices  47.8 us (13%)
  other arithmetic  15.1 us (4%)
  between operations  14.7 us (4%)
    psum x1, blocking collectives, shards(): proj_down, proj_up = lax.psum((partial_down, partial_up), 'tensor')  153 us
    reduce_scatter x1, waiting for transfers between devices, shards(): lax.psum_scatter(term_down, 'dp', scatter_dimension=0, tiled=True)  46.4 us
    gather x1, local copies, waits for them, and re-layouts, shards(): storage_input = padded_x[lookup]  27.4 us
    dot_general x1, matrix products, shards(): lax.dot_general(lax.all_gather(masked, 'tensor', axis=1, tiled=True), key...  21.2 us
    gather x1, local copies, waits for them, and re-layouts, shards(): side_rows = side_slots[target]  19.1 us
    gather x1, local copies, waits for them, and re-layouts, shards(): slot_g = padded_g[lookup]  13.3 us
    psum x1, blocking collectives, shards(): lax.psum((jnp.sum(square_down, axis=1), jnp.sum(square_up, axis=2), jnp.s...  11.9 us
    dot_general x1, matrix products, shards(): jnp.einsum('tcd,tdr->tcr', group_x, every_down, preferred_element_type=jn...  11.1 us
  transfers between devices with their start and end apart: 5, of which 1 were waited for; matrix products, arithmetic and copies ran while one was open for 38% of the time, Pallas kernels for 0%

commit v1 on v0

--- a/solution.py
+++ b/solution.py
@@ -1,6 +1,8 @@
 import jax
 import jax.numpy as jnp
 from jax import lax
+from jax.experimental import pallas as pl
+from jax.experimental.pallas import tpu as pltpu
 from jax.sharding import PartitionSpec as P
 
 adapter_scale = 0.25
@@ -25,7 +27,7 @@
     return (target, lookup)
 
 
-def shards(
+def native_shards(
     activations,
     output_gradient,
     row_tenant,
@@ -110,7 +112,395 @@
     return (input_grad, down_rows, down_cols, up_rows, up_cols, down_update, up_update)
 
 
+LANES = 128
+
+
+def dot(a, b, ca, cb):
+    return lax.dot_general(a, b, (((ca,), (cb,)), ((), ())), preferred_element_type=jnp.float32)
+
+
+def fold_lanes(acc, rank):
+    total = acc
+    for shift in range(rank, LANES, rank):
+        total = total + pltpu.roll(total if shift == rank else acc, shift, 1)
+    return total
+
+
+def project_body(rank, first, scal, x, g, e, *rest):
+    maps, out = rest[:4], rest[-1]
+    rows = x.shape[0]
+    start = pl.program_id(0) * rows
+
+    @pl.when(start < scal[2])
+    def _():
+        part = lax.broadcasted_iota(jnp.int32, (rows, LANES), 1) // rank
+        row = start + lax.broadcasted_iota(jnp.int32, (rows, LANES), 0)
+        sums = []
+        for side, source in ((0, x), (1, g)):
+            acc = jnp.zeros((rows, LANES), jnp.float32)
+            for block in range(2):
+                table = maps[2 * side + block]
+                product = dot(source[...], table[...], 1, 1)
+                for k in range(table.shape[0] // LANES):
+                    hit = e[...] == scal[block] + k * (LANES // rank) + part
+                    acc = acc + jnp.where(hit, product[:, k * LANES : (k + 1) * LANES], 0.0)
+            sums.append(fold_lanes(acc, rank))
+        total = jnp.where(part == 0, sums[0], sums[1])
+        total = jnp.where(row < scal[2], total, 0.0)
+        if not first:
+            total = total + rest[4][...]
+        out[...] = total
+
+    @pl.when(start >= scal[2])
+    def _():
+        out[...] = jnp.zeros_like(out)
+
+
+def project(scal, x, g, e, downs, ups, rank, blocks, prev=None):
+    count_rows, width = x.shape
+    rows = count_rows // blocks
+    kv = g.shape[1]
+    size = downs[0].shape[0]
+
+    def by_row(i, s):
+        return (i, 0)
+
+    def whole(i, s):
+        return (0, 0)
+
+    specs = [
+        pl.BlockSpec((rows, width), by_row),
+        pl.BlockSpec((rows, kv), by_row),
+        pl.BlockSpec((rows, LANES), by_row),
+        pl.BlockSpec((size, width), whole),
+        pl.BlockSpec((size, width), whole),
+        pl.BlockSpec((size, kv), whole),
+        pl.BlockSpec((size, kv), whole),
+    ]
+    args = [x, g, e, *downs, *ups]
+    if prev is not None:
+        specs.append(pl.BlockSpec((rows, LANES), by_row))
+        args.append(prev)
+
+    def kernel(*refs):
+        project_body(rank, prev is None, *refs)
+
+    return pl.pallas_call(
+        kernel,
+        grid_spec=pltpu.PrefetchScalarGridSpec(
+            num_scalar_prefetch=1,
+            grid=(blocks,),
+            in_specs=specs,
+            out_specs=pl.BlockSpec((rows, LANES), by_row),
+        ),
+        out_shape=jax.ShapeDtypeStruct((count_rows, LANES), jnp.float32),
+        name="project",
+    )(scal, *args)
+
+
+def spread(value, e, base, size, rank):
+    part = lax.broadcasted_iota(jnp.int32, value.shape, 1) // rank
+    pieces = []
+    for k in range(size // LANES):
+        hit = e == base + k * (LANES // rank) + part
+        pieces.append(jnp.where(hit, value, 0.0).astype(jnp.bfloat16))
+    return pieces
+
+
+def twice(both, rank):
+    value = both.astype(jnp.float32)
+    part = lax.broadcasted_iota(jnp.int32, value.shape, 1) // rank
+    turned = pltpu.roll(value, rank, 1)
+    return (jnp.where(part == 0, value, turned), jnp.where(part == 0, turned, value))
+
+
+def gradients(scal, both, e, x, g, size, rank):
+    count_rows, width = x.shape
+    kv = g.shape[1]
+    tiles = width // kv
+
+    def kernel(scal, both, e, x, g, sent, kept, up_wide, down_wide):
+        j = pl.program_id(0)
+
+        @pl.when(j == 0)
+        def _():
+            d, u = twice(both[...], rank)
+            for block in range(2):
+                for wide, value in ((up_wide, u), (down_wide, d)):
+                    for k, piece in enumerate(spread(value, e[...], scal[block], size, rank)):
+                        at = block * size + k * LANES
+                        wide[:, at : at + LANES] = piece
+
+        def put(result):
+            result = adapter_scale * result
+            sent[...] = result[:size].astype(jnp.bfloat16)
+            kept[...] = result[size:]
+
+        @pl.when(j < tiles)
+        def _():
+            put(dot(up_wide[...], x[...], 0, 0))
+
+        @pl.when(j == tiles)
+        def _():
+            put(dot(down_wide[...], g[...], 0, 0))
+
+    return pl.pallas_call(
+        kernel,
+        grid_spec=pltpu.PrefetchScalarGridSpec(
+            num_scalar_prefetch=1,
+            grid=(tiles + 1,),
+            in_specs=[
+                pl.BlockSpec((count_rows, LANES), lambda j, s: (0, 0)),
+                pl.BlockSpec((count_rows, LANES), lambda j, s: (0, 0)),
+                pl.BlockSpec((count_rows, kv), lambda j, s: (0, jnp.minimum(j, tiles - 1))),
+                pl.BlockSpec((count_rows, kv), lambda j, s: (0, 0)),
+            ],
+            out_specs=[
+                pl.BlockSpec((size, kv), lambda j, s: (0, j)),
+                pl.BlockSpec((size, kv), lambda j, s: (0, j)),
+            ],
+            scratch_shapes=[
+                pltpu.VMEM((count_rows, 2 * size), jnp.bfloat16),
+                pltpu.VMEM((count_rows, 2 * size), jnp.bfloat16),
+            ],
+        ),
+        out_shape=[
+            jax.ShapeDtypeStruct((size, width + kv), jnp.bfloat16),
+            jax.ShapeDtypeStruct((size, width + kv), jnp.float32),
+        ],
+        name="gradients",
+    )(scal, both, e, x, g)
+
+
+def input_chunk(scal, chunk, chunks, g, near, both, e, weight, downs, out, rank):
+    count_rows, kv = g.shape
+    width = weight.shape[0]
+    rows = count_rows // chunks
+    size = downs[0].shape[0]
+    tiles = width // kv
+
+    def kernel(scal, own, left, right, far, wrap, both, e, w0, w1, w2, w3, *rest):
+        maps, result, wide = rest[: len(downs)], rest[-2], rest[-1]
+        j = pl.program_id(0)
+        start = chunk * rows
+
+        @pl.when((j == 0) & (start < scal[5]))
+        def _():
+            u = twice(both[...], rank)[1]
+            for block in range(len(downs)):
+                for k, piece in enumerate(spread(u, e[...], scal[6 + block], size, rank)):
+                    at = block * size + k * LANES
+                    wide[:, at : at + LANES] = piece
+
+        @pl.when(start < scal[5])
+        def _():
+            from_left = jnp.where(scal[4] < 0, wrap[...], left[...])
+            from_right = jnp.where(scal[4] > 0, wrap[...], right[...])
+            acc = dot(own[...], w0[...], 1, 1)
+            acc = acc + dot(from_left, w1[...], 1, 1)
+            acc = acc + dot(from_right, w2[...], 1, 1)
+            acc = acc + dot(far[...], w3[...], 1, 1)
+            side = jnp.zeros_like(acc)
+            for block, table in enumerate(maps):
+                side = side + dot(wide[:, block * size : (block + 1) * size], table[...], 1, 0)
+            side = (adapter_scale * side).astype(jnp.bfloat16).astype(jnp.float32)
+            row = start + lax.broadcasted_iota(jnp.int32, acc.shape, 0)
+            result[...] = jnp.where(row < scal[5], acc + side, 0.0).astype(jnp.bfloat16)
+
+        @pl.when(start >= scal[5])
+        def _():
+            result[...] = jnp.zeros_like(result)
+
+    def at_chunk(j, s):
+        return (chunk, 0)
+
+    def whole(j, s):
+        return (0, 0)
+
+    def weight_spec(slot):
+        return pl.BlockSpec((kv, kv), lambda j, s: (j, s[slot]))
+
+    specs = [pl.BlockSpec((rows, kv), at_chunk)]
+    specs += [pl.BlockSpec((rows, kv), whole)] * 4
+    specs += [pl.BlockSpec((rows, LANES), at_chunk)] * 2
+    specs += [weight_spec(k) for k in range(4)]
+    specs += [pl.BlockSpec((size, kv), lambda j, s: (0, j))] * len(downs)
+    args = [scal, g, *near, both, e, weight, weight, weight, weight, *downs]
+    aliases = {}
+    if out is not None:
+        specs.append(pl.BlockSpec(memory_space=pl.ANY))
+        aliases = {len(args): 0}
+        args.append(out)
+    return pl.pallas_call(
+        kernel,
+        grid_spec=pltpu.PrefetchScalarGridSpec(
+            num_scalar_prefetch=1,
+            grid=(tiles,),
+            in_specs=specs,
+            out_specs=pl.BlockSpec((rows, kv), lambda j, s: (chunk, j)),
+            scratch_shapes=[pltpu.VMEM((rows, len(downs) * size), jnp.bfloat16)],
+        ),
+        out_shape=jax.ShapeDtypeStruct((count_rows, width), jnp.bfloat16),
+        input_output_aliases=aliases,
+        name="input_chunk",
+    )(*args)
+
+
+def permute_shards(
+    activations,
+    output_gradient,
+    row_tenant,
+    group_row_count,
+    tenant_storage_entry,
+    key_value_weight,
+    adapter_down_maps,
+    adapter_up_maps,
+    down_row_factor,
+    down_column_factor,
+    up_row_factor,
+    up_column_factor,
+):
+    group_total = lax.axis_size("dp")
+    line = lax.axis_size("tensor")
+    here = lax.axis_index("tensor")
+    group = lax.axis_index("dp")
+    owned, width, rank = adapter_down_maps.shape
+    kv = adapter_up_maps.shape[2]
+    size = owned * rank
+    count_rows = activations.shape[0]
+    full_width = width * line
+    pair_width = kv * line
+    chunks = line
+    rows = count_rows // chunks
+    x, g = activations, output_gradient
+
+    sibling = [(i, i ^ 1) for i in range(group_total)]
+    across = [(i, i ^ 2) for i in range(group_total)]
+    rightward = [(i, i + 1) for i in range(line - 1)]
+    leftward = [(i + 1, i) for i in range(line - 1)]
+    half = [(i, (i + line // 2) % line) for i in range(line)]
+    ends = [(line - 2, line - 1), (1, 0)]
+
+    def shift(value, step):
+        perm = [(i, (i + step) % line) for i in range(line)]
+        return lax.ppermute(value, "tensor", perm)
+
+    own_down = jnp.swapaxes(adapter_down_maps, 1, 2).reshape(size, width)
+    own_up = adapter_up_maps.reshape(size, kv)
+    far_down = lax.ppermute(own_down, "dp", across)
+    far_up = lax.ppermute(own_up, "dp", across)
+    side_down = lax.ppermute(own_down, "dp", sibling)
+    side_up = lax.ppermute(own_up, "dp", sibling)
+    cross_down = lax.ppermute(far_down, "dp", sibling)
+    cross_up = lax.ppermute(far_up, "dp", sibling)
+
+    near = []
+    for c in range(chunks):
+        piece = g[c * rows : (c + 1) * rows]
+        far = lax.ppermute(piece, "tensor", half)
+        left = lax.ppermute(piece, "tensor", rightward)
+        right = lax.ppermute(piece, "tensor", leftward)
+        wrap = lax.ppermute(far, "tensor", ends)
+        near.append((left, right, far, wrap))
+
+    entry_count = tenant_storage_entry.shape[0]
+    named = row_tenant == jnp.arange(entry_count, dtype=jnp.int32)[None, :]
+    entry = jnp.sum(jnp.where(named, tenant_storage_entry[None, :], 0), axis=1, keepdims=True)
+    e = jnp.broadcast_to(entry, (count_rows, LANES))
+    count = group_row_count[0]
+    base = [owned * group, owned * (group ^ 1), owned * (group ^ 2), owned * (group ^ 3)]
+
+    def table(*values):
+        return jnp.stack([jnp.asarray(v, jnp.int32) for v in values])
+
+    partial = project(
+        table(base[0], base[1], count), x, g, e, (own_down, side_down), (own_up, side_up), rank, chunks
+    )
+    partial = project(
+        table(base[2], base[3], count),
+        x,
+        g,
+        e,
+        (far_down, cross_down),
+        (far_up, cross_up),
+        rank,
+        chunks,
+        partial,
+    )
+
+    def rows_of(index):
+        return lax.dynamic_slice_in_dim(partial, index * rows, rows, 0)
+
+    total = rows_of(here)
+    for step in range(1, line):
+        total = total + shift(rows_of((here + step) % line), step)
+    rounded = total.astype(jnp.bfloat16)
+    both = jnp.zeros((count_rows, LANES), jnp.bfloat16)
+    for step in range(line):
+        piece = shift(rounded, step) if step else rounded
+        both = lax.dynamic_update_slice_in_dim(both, piece, (here - step) % line * rows, 0)
+
+    sent, kept_far = gradients(table(base[3], base[2]), both, e, x, g, size, rank)
+    got = lax.ppermute(sent, "dp", sibling)
+    sent, kept = gradients(table(base[1], base[0]), both, e, x, g, size, rank)
+    kept = kept + lax.ppermute(sent, "dp", sibling).astype(jnp.float32)
+    outgoing = (kept_far + got.astype(jnp.float32)).astype(jnp.bfloat16)
+    grad = kept + lax.ppermute(outgoing, "dp", across).astype(jnp.float32)
+
+    down_gradient = grad[:, :width].reshape(owned, rank, width)
+    up_gradient = grad[:, width:].reshape(owned, rank, kv)
+    square_down = down_gradient * down_gradient + tiny_floor
+    square_up = up_gradient * up_gradient + tiny_floor
+    down_rows = decay_rate * down_row_factor + (1.0 - decay_rate) * jnp.mean(square_down, axis=1)
+    up_cols = decay_rate * up_column_factor + (1.0 - decay_rate) * jnp.mean(square_up, axis=1)
+    spill = jnp.zeros((owned, rank), jnp.float32)
+    stats = jnp.concatenate(
+        [
+            jnp.concatenate([jnp.sum(square_down, axis=2), jnp.sum(square_up, axis=2)], axis=1),
+            jnp.concatenate([spill + jnp.sum(down_rows, axis=1)[:, None], spill], axis=1),
+        ],
+        axis=0,
+    )
+    sums = stats
+    for step in range(1, line):
+        sums = sums + shift(stats, step)
+    column_total, row_total = sums[:owned, :rank], sums[:owned, rank:]
+    rows_sum = sums[owned:, :1]
+    down_cols = decay_rate * down_column_factor + (1.0 - decay_rate) * (column_total / full_width)
+    up_rows = decay_rate * up_row_factor + (1.0 - decay_rate) * (row_total / pair_width)
+    second_down = (
+        down_cols[:, :, None] * down_rows[:, None, :] / (rows_sum / full_width)[:, :, None]
+    )
+    second_up = up_rows[:, :, None] * up_cols[:, None, :] / jnp.mean(up_rows, axis=1)[:, None, None]
+    down_update = jnp.swapaxes(down_gradient * lax.rsqrt(second_down), 1, 2)
+    up_update = up_gradient * lax.rsqrt(second_up)
+
+    wrapped = jnp.where(here == 0, -1, jnp.where(here == line - 1, 1, 0))
+    scal = table(
+        here,
+        (here - 1) % line,
+        (here + 1) % line,
+        (here + 2) % line,
+        wrapped,
+        count,
+        *base,
+    )
+    input_grad = None
+    for c in range(chunks):
+        maps = (own_down, side_down, far_down, cross_down)
+        input_grad = input_chunk(
+            scal, c, chunks, g, near[c], both, e, key_value_weight, maps, input_grad, rank
+        )
+    return (input_grad, down_rows, down_cols, up_rows, up_cols, down_update, up_update)
+
+
+def staged(*args):
+    return permute_shards(*args)
+
+
 def solution(mesh):
+    small = mesh.shape["tensor"] == 4 and mesh.shape["dp"] == 4
+    body = staged if small else native_shards
     in_specs = (
         P(("rep", "dp"), "tensor"),
         P(("rep", "dp"), "tensor"),
@@ -134,4 +524,4 @@
         P(("rep", "dp"), "tensor", None),
         P(("rep", "dp"), None, "tensor"),
     )
-    return jax.shard_map(shards, mesh=mesh, in_specs=in_specs, out_specs=out_specs, check_vma=False)
+    return jax.shard_map(body, mesh=mesh, in_specs=in_specs, out_specs=out_specs, check_vma=False)

time: 380 us -> 293 us (0.77)
  the two profiles are of different devices: /device:TPU:0 before, /device:TPU:1 now
where the time goes in v1:
time: 293 us; the launch traced here: 292 us
  waiting for transfers between devices  101 us (34%)
  Pallas kernels  85.4 us (29%)
  starting transfers between devices  81.7 us (28%)
  other arithmetic  13.4 us (5%)
  local copies, waits for them, and re-layouts  9.14 us (3%)
    pallas_call x4, Pallas kernels, input_chunk(): pl.pallas_call(kernel, grid_spec=pltpu.PrefetchScalarGridSpec(num_scalar_...  44.9 us
    ppermute x4, starting transfers between devices, permute_shards(): left = lax.ppermute(piece, 'tensor', rightward)  28.5 us
    ppermute x9, waiting for transfers between devices, shift(): return lax.ppermute(value, 'tensor', perm)  22.2 us
    ppermute x1, waiting for transfers between devices, permute_shards(): far_down = lax.ppermute(own_down, 'dp', across)  22.1 us
    pallas_call x2, Pallas kernels, gradients(): pl.pallas_call(kernel, grid_spec=pltpu.PrefetchScalarGridSpec(num_scalar_...  21.5 us
    ppermute x4, waiting for transfers between devices, permute_shards(): wrap = lax.ppermute(far, 'tensor', ends)  21.4 us
    ppermute x4, waiting for transfers between devices, permute_shards(): far = lax.ppermute(piece, 'tensor', half)  21.2 us
    ppermute x4, starting transfers between devices, permute_shards(): far = lax.ppermute(piece, 'tensor', half)  19.9 us
  transfers between devices with their start and end apart: 34, of which 17 were waited for; matrix products, arithmetic and copies ran while one was open for 3% of the time, Pallas kernels for 22%

profile of v1, /device:TPU:1, one launch (start us, length us, event | category | flops | bytes accessed | tf_op | source)
XLA Modules:
  0.0 292.3 jit_solution(12667691632163367925)
XLA Ops:
  3.7 22.1 %collective-permute-done.4.refs_4_.rest_2_ = bf16[256,2048]{1,0:T(8,128)(2,1)S(1)} collective-permute-done((bf16[256,2048]{1,0:T(8,128)(2,1)}, bf16[256,2048]{1,0:T(8,128)(2,1)S(1)}, u32[]{:S(2)}, u32[]{:S(2)}) %collective-permute-start.4) | collective-permute-done | bytes 1048608 | tf_op jit(solution)/shard_map/ppermute | solution.py:390
  28.8 6.3 %collective-permute-done.6.refs_6_ = bf16[256,512]{1,0:T(8,128)(2,1)S(1)} collective-permute-done((bf16[256,512]{1,0:T(8,128)(2,1)}, bf16[256,512]{1,0:T(8,128)(2,1)S(1)}, u32[]{:S(2)}, u32[]{:S(2)}) %collective-permute-start.6) | collective-permute-done | bytes 262176 | tf_op jit(solution)/shard_map/ppermute | solution.py:391
  40.1 9.5 %project.2.refs_8_ = f32[1536,128]{1,0:T(8,128)} custom-call(s32[3]{0:T(128)} %get-tuple-element.30.refs_0_, bf16[1536,2048]{1,0:T(8,128)(2,1)} %x.5, bf16[1536,512]{1,0:T(8,128)(2,1)} %g.3, s32[1536,128]{1,0:T(8,128)} %broadcast_in_dim.19.refs_3_.e, bf16[256,2048]{1,0:T(8,128)(2,1)} %bitcast.23, bf16[256,2048]{1,0:T(8,128)(2,1)} %copy-done.2, ...), custom_call_target="tpu_custom_call" | custom-call | tf_op jit(solution)/shard_map/project/pallas_call | solution.py:188
  50.3 9.5 %project.3 = f32[1536,128]{1,0:T(8,128)} custom-call(s32[3]{0:T(128)} %get-tuple-element.29.refs_0_, bf16[1536,2048]{1,0:T(8,128)(2,1)} %x.5, bf16[1536,512]{1,0:T(8,128)(2,1)} %g.3, s32[1536,128]{1,0:T(8,128)} %broadcast_in_dim.19.refs_3_.e, bf16[256,2048]{1,0:T(8,128)(2,1)} %copy-done.1, bf16[256,2048]{1,0:T(8,128)(2,1)} %collective-permute-done.5.refs_5_.rest_3_, ...), custom_call_target="tpu_custom_call" | custom-call | tf_op jit(solution)/shard_map/project/pallas_call | solution.py:188
  61.0 3.6 %collective-permute-start.12 = (f32[384,128]{1,0:T(8,128)S(1)}, f32[384,128]{1,0:T(8,128)S(1)}, u32[]{:S(2)}, u32[]{:S(2)}) collective-permute-start(f32[384,128]{1,0:T(8,128)S(1)} %get-tuple-element.26), channel_id=1, source_target_pairs={{0,3},{1,0},{2,1},{3,2},{4,7},{5,4},{6,5},{7,6},{8,11},{9,8},{10,9... | collective-permute-start | bytes 589832 | tf_op jit(solution)/shard_map/ppermute | solution.py:386
  65.0 4.3 %collective-permute-done.12 = f32[384,128]{1,0:T(8,128)S(1)} collective-permute-done((f32[384,128]{1,0:T(8,128)S(1)}, f32[384,128]{1,0:T(8,128)S(1)}, u32[]{:S(2)}, u32[]{:S(2)}) %collective-permute-start.12) | collective-permute-done | bytes 196640 | tf_op jit(solution)/shard_map/ppermute | solution.py:386
  69.4 10.2 %collective-permute-done.11 = f32[384,128]{1,0:T(8,128)S(1)} collective-permute-done((f32[384,128]{1,0:T(8,128)S(1)}, f32[384,128]{1,0:T(8,128)S(1)}, u32[]{:S(2)}, u32[]{:S(2)}) %collective-permute-start.11) | collective-permute-done | bytes 196640 | tf_op jit(solution)/shard_map/ppermute | solution.py:386
  87.0 4.5 %collective-permute-done.14 = bf16[384,128]{1,0:T(8,128)(2,1)S(1)} collective-permute-done((bf16[384,128]{1,0:T(8,128)(2,1)S(1)}, bf16[384,128]{1,0:T(8,128)(2,1)S(1)}, u32[]{:S(2)}, u32[]{:S(2)}) %collective-permute-start.14) | collective-permute-done | bytes 98336 | tf_op jit(solution)/shard_map/ppermute | solution.py:386
  92.3 10.8 %gradients.3 = (bf16[256,2560]{1,0:T(8,128)(2,1)}, f32[256,2560]{1,0:T(8,128)}) custom-call(s32[2]{0:T(128)} %get-tuple-element.32.scal, bf16[1536,128]{1,0:T(8,128)(2,1)} %copy-done.3, s32[1536,128]{1,0:T(8,128)} %broadcast_in_dim.19.refs_3_.e, bf16[1536,2048]{1,0:T(8,128)(2,1)} %x.5, bf16[1536,512]{1,0:T(8,128)(2,1)} %g.3), custom_call_target="tpu_custom_call" | custom-call | tf_op jit(solution)/shard_map/gradients/pallas_call | solution.py:247
  106.4 4.6 %collective-permute-start.16 = (bf16[384,512]{1,0:T(8,128)(2,1)}, bf16[384,512]{1,0:T(8,128)(2,1)S(1)}, u32[]{:S(2)}, u32[]{:S(2)}) collective-permute-start(bf16[384,512]{1,0:T(8,128)(2,1)} %get-tuple-element.23), channel_id=1, source_target_pairs={{0,1},{1,2},{2,3},{4,5},{5,6},{6,7},{8,9},{9,10},{10,11},{12,13},{... | collective-permute-start | bytes 1179656 | tf_op jit(solution)/shard_map/ppermute | solution.py:401
  114.2 10.7 %gradients.2 = (bf16[256,2560]{1,0:T(8,128)(2,1)}, f32[256,2560]{1,0:T(8,128)}) custom-call(s32[2]{0:T(128)} %get-tuple-element.31.scal, bf16[1536,128]{1,0:T(8,128)(2,1)} %copy-done.3, s32[1536,128]{1,0:T(8,128)} %broadcast_in_dim.19.refs_3_.e, bf16[1536,2048]{1,0:T(8,128)(2,1)} %x.5, bf16[1536,512]{1,0:T(8,128)(2,1)} %g.3), custom_call_target="tpu_custom_call" | custom-call | tf_op jit(solution)/shard_map/gradients/pallas_call | solution.py:247
  125.1 3.1 %collective-permute-start.20 = (bf16[384,512]{1,0:T(8,128)(2,1)}, bf16[384,512]{1,0:T(8,128)(2,1)S(1)}, u32[]{:S(2)}, u32[]{:S(2)}) collective-permute-start(bf16[384,512]{1,0:T(8,128)(2,1)} %get-tuple-element.22), channel_id=1, source_target_pairs={{0,1},{1,2},{2,3},{4,5},{5,6},{6,7},{8,9},{9,10},{10,11},{12,13},{... | collective-permute-start | bytes 1179656 | tf_op jit(solution)/shard_map/ppermute | solution.py:401
  129.5 16.5 %collective-permute-start.22 = (bf16[384,512]{1,0:T(8,128)(2,1)}, bf16[384,512]{1,0:T(8,128)(2,1)S(1)}, u32[]{:S(2)}, u32[]{:S(2)}) collective-permute-start(bf16[384,512]{1,0:T(8,128)(2,1)} %get-tuple-element.22), channel_id=1, source_target_pairs={{0,2},{1,3},{2,0},{3,1},{4,6},{5,7},{6,4},{7,5},{8,10},{9,11},{10,... | collective-permute-start | bytes 1179656 | tf_op jit(solution)/shard_map/ppermute | solution.py:400
  150.5 18.8 %collective-permute-start.24 = (bf16[384,512]{1,0:T(8,128)(2,1)S(1)}, bf16[384,512]{1,0:T(8,128)(2,1)S(1)}, u32[]{:S(2)}, u32[]{:S(2)}) collective-permute-start(bf16[384,512]{1,0:T(8,128)(2,1)S(1)} %copy-done.18), channel_id=1, source_target_pairs={{0,1},{1,2},{2,3},{4,5},{5,6},{6,7},{8,9},{9,10},{10,11},{12,13},{... | collective-permute-start | bytes 1179656 | tf_op jit(solution)/shard_map/ppermute | solution.py:401
  170.7 5.0 %collective-permute-done.22.far = bf16[384,512]{1,0:T(8,128)(2,1)S(1)} collective-permute-done((bf16[384,512]{1,0:T(8,128)(2,1)}, bf16[384,512]{1,0:T(8,128)(2,1)S(1)}, u32[]{:S(2)}, u32[]{:S(2)}) %collective-permute-start.22) | collective-permute-done | bytes 393248 | tf_op jit(solution)/shard_map/ppermute | solution.py:400
  178.6 5.9 %collective-permute-done.25.right = bf16[384,512]{1,0:T(8,128)(2,1)S(1)} collective-permute-done((bf16[384,512]{1,0:T(8,128)(2,1)S(1)}, bf16[384,512]{1,0:T(8,128)(2,1)S(1)}, u32[]{:S(2)}, u32[]{:S(2)}) %collective-permute-start.25) | collective-permute-done | bytes 393248 | tf_op jit(solution)/shard_map/ppermute | solution.py:402
  185.8 14.9 %collective-permute-done.26.far = bf16[384,512]{1,0:T(8,128)(2,1)S(1)} collective-permute-done((bf16[384,512]{1,0:T(8,128)(2,1)S(1)}, bf16[384,512]{1,0:T(8,128)(2,1)S(1)}, u32[]{:S(2)}, u32[]{:S(2)}) %collective-permute-start.26) | collective-permute-done | bytes 393248 | tf_op jit(solution)/shard_map/ppermute | solution.py:400
  201.9 7.9 %collective-permute-done.19.wrap = bf16[384,512]{1,0:T(8,128)(2,1)S(1)} collective-permute-done((bf16[384,512]{1,0:T(8,128)(2,1)}, bf16[384,512]{1,0:T(8,128)(2,1)S(1)}, u32[]{:S(2)}, u32[]{:S(2)}) %collective-permute-start.19) | collective-permute-done | bytes 393248 | tf_op jit(solution)/shard_map/ppermute | solution.py:403
  211.9 6.4 %collective-permute-done.23.wrap = bf16[384,512]{1,0:T(8,128)(2,1)S(1)} collective-permute-done((bf16[384,512]{1,0:T(8,128)(2,1)S(1)}, bf16[384,512]{1,0:T(8,128)(2,1)S(1)}, u32[]{:S(2)}, u32[]{:S(2)}) %collective-permute-start.23) | collective-permute-done | bytes 393248 | tf_op jit(solution)/shard_map/ppermute | solution.py:403
  219.5 7.1 %collective-permute-done.27.wrap = bf16[384,512]{1,0:T(8,128)(2,1)S(1)} collective-permute-done((bf16[384,512]{1,0:T(8,128)(2,1)S(1)}, bf16[384,512]{1,0:T(8,128)(2,1)S(1)}, u32[]{:S(2)}, u32[]{:S(2)}) %collective-permute-start.27) | collective-permute-done | bytes 393248 | tf_op jit(solution)/shard_map/ppermute | solution.py:403
  229.6 11.2 %input_chunk.4.rest_4_ = bf16[1536,2048]{1,0:T(8,128)(2,1)} custom-call(s32[10]{0:T(128)} %stack.59.scal, bf16[1536,512]{1,0:T(8,128)(2,1)} %g.3, bf16[384,512]{1,0:T(8,128)(2,1)} %copy-done.12, bf16[384,512]{1,0:T(8,128)(2,1)} %copy-done.13, bf16[384,512]{1,0:T(8,128)(2,1)} %copy-done.15, bf16[384,512]{1,0:T(8,128)(2,1)} %copy-done.17, ...), custom_call_target="tpu_custom_call" | custom-call | tf_op jit(solution)/shard_map/input_chunk/pallas_call | solution.py:334
  240.8 11.2 %input_chunk.5.rest_4_ = bf16[1536,2048]{1,0:T(8,128)(2,1)} custom-call(s32[10]{0:T(128)} %stack.59.scal, bf16[1536,512]{1,0:T(8,128)(2,1)} %g.3, bf16[384,512]{1,0:T(8,128)(2,1)} %copy-done.9, bf16[384,512]{1,0:T(8,128)(2,1)} %copy-done.10, bf16[384,512]{1,0:T(8,128)(2,1)} %copy-done.11, ...), custom_call_target="tpu_custom_call", output_to_operand_aliasing={{}: (16, {})} | custom-call | tf_op jit(solution)/shard_map/input_chunk/pallas_call | solution.py:334
  252.1 11.2 %input_chunk.6.rest_4_ = bf16[1536,2048]{1,0:T(8,128)(2,1)} custom-call(s32[10]{0:T(128)} %stack.59.scal, bf16[1536,512]{1,0:T(8,128)(2,1)} %g.3, bf16[384,512]{1,0:T(8,128)(2,1)} %copy-done.8, bf16[384,512]{1,0:T(8,128)(2,1)} %collective-permute-done.17.right, bf16[384,512]{1,0:T(8,128)(2,1)} %collective-permute-done.18.far, ...), custom_call_target="tpu_custom_call", output_to_operand_aliasing={{}: (16, {})} | custom-call | tf_op jit(solution)/shard_map/input_chunk/pallas_call | solution.py:334
  263.3 11.2 %input_chunk.7 = bf16[1536,2048]{1,0:T(8,128)(2,1)} custom-call(s32[10]{0:T(128)} %stack.59.scal, bf16[1536,512]{1,0:T(8,128)(2,1)} %g.3, bf16[384,512]{1,0:T(8,128)(2,1)} %collective-permute-done.left, bf16[384,512]{1,0:T(8,128)(2,1)} %collective-permute-done.1.right, bf16[384,512]{1,0:T(8,128)(2,1)} %copy-done.7, ...), custom_call_target="tpu_custom_call", output_to_operand_aliasing={{}: (16, {})} | custom-call | tf_op jit(solution)/shard_map/input_chunk/pallas_call | solution.py:334
  (143 shorter events, 63.9 us)
Async XLA Ops:
  0.6 25.2 %collective-permute-start.4 = (bf16[256,2048]{1,0:T(8,128)(2,1)}, bf16[256,2048]{1,0:T(8,128)(2,1)S(1)}, u32[]{:S(2)}, u32[]{:S(2)}) collective-permute-start(bf16[256,2048]{1,0:T(8,128)(2,1)} %bitcast.21), channel_id=1, source_target_pairs={{0,8},{4,12},{8,0},{12,4},{1,9},{5,13},{9,1},{13,5},{2,10},{6,14},... | collective-permute-start | bytes 3145736 | tf_op jit(solution)/shard_map/ppermute | solution.py:390
  2.7 36.0 %collective-permute-start.8 = (bf16[256,2048]{1,0:T(8,128)(2,1)}, bf16[256,2048]{1,0:T(8,128)(2,1)S(1)}, u32[]{:S(2)}, u32[]{:S(2)}) collective-permute-start(bf16[256,2048]{1,0:T(8,128)(2,1)} %bitcast.22), channel_id=1, source_target_pairs={{0,4},{4,0},{8,12},{12,8},{1,5},{5,1},{9,13},{13,9},{2,6},{6,2},{1... | collective-permute-start | bytes 3145736 | tf_op jit(solution)/shard_map/ppermute | solution.py:392
  25.8 23.8 %collective-permute-start.5 = (bf16[256,2048]{1,0:T(8,128)(2,1)S(1)}, bf16[256,2048]{1,0:T(8,128)(2,1)}, u32[]{:S(2)}, u32[]{:S(2)}) collective-permute-start(bf16[256,2048]{1,0:T(8,128)(2,1)S(1)} %collective-permute-done.4.refs_4_.rest_2_), channel_id=1, source_target_pairs={{0,4},{4,0},{8,12},{12,8},{1,5},{5,1},{9,13},{13,9},{2,6},{6,2},{1... | collective-permute-start | bytes 3145736 | tf_op jit(solution)/shard_map/ppermute | solution.py:394
  64.6 15.0 %collective-permute-start.11 = (f32[384,128]{1,0:T(8,128)S(1)}, f32[384,128]{1,0:T(8,128)S(1)}, u32[]{:S(2)}, u32[]{:S(2)}) collective-permute-start(f32[384,128]{1,0:T(8,128)S(1)} %get-tuple-element.27), channel_id=1, source_target_pairs={{0,2},{1,3},{2,0},{3,1},{4,6},{5,7},{6,4},{7,5},{8,10},{9,11},{10,... | collective-permute-start | bytes 589832 | tf_op jit(solution)/shard_map/ppermute | solution.py:386
  64.6 15.0 %collective-permute-start.10 = (f32[384,128]{1,0:T(8,128)S(1)}, f32[384,128]{1,0:T(8,128)S(1)}, u32[]{:S(2)}, u32[]{:S(2)}) collective-permute-start(f32[384,128]{1,0:T(8,128)S(1)} %get-tuple-element.25), channel_id=1, source_target_pairs={{0,1},{1,2},{2,3},{3,0},{4,5},{5,6},{6,7},{7,4},{8,9},{9,10},{10,1... | collective-permute-start | bytes 589832 | tf_op jit(solution)/shard_map/ppermute | solution.py:386
  103.1 26.3 %collective-permute-start.29 = (bf16[256,2560]{1,0:T(8,128)(2,1)}, bf16[256,2560]{1,0:T(8,128)(2,1)}, u32[]{:S(2)}, u32[]{:S(2)}) collective-permute-start(bf16[256,2560]{1,0:T(8,128)(2,1)} %get-tuple-element.14), channel_id=1, source_target_pairs={{0,4},{4,0},{8,12},{12,8},{1,5},{5,1},{9,13},{13,9},{2,6},{6,2},{1... | collective-permute-start | bytes 3932168 | tf_op jit(solution)/shard_map/ppermute | solution.py:444
  104.8 20.2 %collective-permute-start.2 = (bf16[384,512]{1,0:T(8,128)(2,1)}, bf16[384,512]{1,0:T(8,128)(2,1)S(1)}, u32[]{:S(2)}, u32[]{:S(2)}) collective-permute-start(bf16[384,512]{1,0:T(8,128)(2,1)} %get-tuple-element.24), channel_id=1, source_target_pairs={{0,2},{1,3},{2,0},{3,1},{4,6},{5,7},{6,4},{7,5},{8,10},{9,11},{10,... | collective-permute-start | bytes 1179656 | tf_op jit(solution)/shard_map/ppermute | solution.py:400
  106.4 21.7 %collective-permute-start.16 = (bf16[384,512]{1,0:T(8,128)(2,1)}, bf16[384,512]{1,0:T(8,128)(2,1)S(1)}, u32[]{:S(2)}, u32[]{:S(2)}) collective-permute-start(bf16[384,512]{1,0:T(8,128)(2,1)} %get-tuple-element.23), channel_id=1, source_target_pairs={{0,1},{1,2},{2,3},{4,5},{5,6},{6,7},{8,9},{9,10},{10,11},{12,13},{... | collective-permute-start | bytes 1179656 | tf_op jit(solution)/shard_map/ppermute | solution.py:401
  111.0 37.7 %collective-permute-start.17 = (bf16[384,512]{1,0:T(8,128)(2,1)}, bf16[384,512]{1,0:T(8,128)(2,1)}, u32[]{:S(2)}, u32[]{:S(2)}) collective-permute-start(bf16[384,512]{1,0:T(8,128)(2,1)} %get-tuple-element.23), channel_id=1, source_target_pairs={{1,0},{2,1},{3,2},{5,4},{6,5},{7,6},{9,8},{10,9},{11,10},{13,12},{... | collective-permute-start | bytes 1179656 | tf_op jit(solution)/shard_map/ppermute | solution.py:402
  112.3 38.2 %collective-permute-start.18 = (bf16[384,512]{1,0:T(8,128)(2,1)}, bf16[384,512]{1,0:T(8,128)(2,1)}, u32[]{:S(2)}, u32[]{:S(2)}) collective-permute-start(bf16[384,512]{1,0:T(8,128)(2,1)} %get-tuple-element.23), channel_id=1, source_target_pairs={{0,2},{1,3},{2,0},{3,1},{4,6},{5,7},{6,4},{7,5},{8,10},{9,11},{10,... | collective-permute-start | bytes 1179656 | tf_op jit(solution)/shard_map/ppermute | solution.py:400
  125.1 25.5 %collective-permute-start.20 = (bf16[384,512]{1,0:T(8,128)(2,1)}, bf16[384,512]{1,0:T(8,128)(2,1)S(1)}, u32[]{:S(2)}, u32[]{:S(2)}) collective-permute-start(bf16[384,512]{1,0:T(8,128)(2,1)} %get-tuple-element.22), channel_id=1, source_target_pairs={{0,1},{1,2},{2,3},{4,5},{5,6},{6,7},{8,9},{9,10},{10,11},{12,13},{... | collective-permute-start | bytes 1179656 | tf_op jit(solution)/shard_map/ppermute | solution.py:401
  128.2 41.2 %collective-permute-start.21 = (bf16[384,512]{1,0:T(8,128)(2,1)}, bf16[384,512]{1,0:T(8,128)(2,1)S(1)}, u32[]{:S(2)}, u32[]{:S(2)}) collective-permute-start(bf16[384,512]{1,0:T(8,128)(2,1)} %get-tuple-element.22), channel_id=1, source_target_pairs={{1,0},{2,1},{3,2},{5,4},{6,5},{7,6},{9,8},{10,9},{11,10},{13,12},{... | collective-permute-start | bytes 1179656 | tf_op jit(solution)/shard_map/ppermute | solution.py:402
  129.5 46.2 %collective-permute-start.22 = (bf16[384,512]{1,0:T(8,128)(2,1)}, bf16[384,512]{1,0:T(8,128)(2,1)S(1)}, u32[]{:S(2)}, u32[]{:S(2)}) collective-permute-start(bf16[384,512]{1,0:T(8,128)(2,1)} %get-tuple-element.22), channel_id=1, source_target_pairs={{0,2},{1,3},{2,0},{3,1},{4,6},{5,7},{6,4},{7,5},{8,10},{9,11},{10,... | collective-permute-start | bytes 1179656 | tf_op jit(solution)/shard_map/ppermute | solution.py:400
  148.7 125.9 %collective-permute-start.28 = (bf16[256,2560]{1,0:T(8,128)(2,1)}, bf16[256,2560]{1,0:T(8,128)(2,1)S(1)}, u32[]{:S(2)}, u32[]{:S(2)}) collective-permute-start(bf16[256,2560]{1,0:T(8,128)(2,1)} %get-tuple-element.12), channel_id=1, source_target_pairs={{0,4},{4,0},{8,12},{12,8},{1,5},{5,1},{9,13},{13,9},{2,6},{6,2},{1... | collective-permute-start | bytes 3932168 | tf_op jit(solution)/shard_map/ppermute | solution.py:446
  150.5 124.1 %collective-permute-start.30 = (bf16[256,2560]{1,0:T(8,128)(2,1)}, bf16[256,2560]{1,0:T(8,128)(2,1)S(1)}, u32[]{:S(2)}, u32[]{:S(2)}) collective-permute-start(bf16[256,2560]{1,0:T(8,128)(2,1)} %add_convert_fusion), channel_id=1, source_target_pairs={{0,8},{4,12},{8,0},{12,4},{1,9},{5,13},{9,1},{13,5},{2,10},{6,14},... | collective-permute-start | bytes 3932168 | tf_op jit(solution)/shard_map/ppermute | solution.py:448
  150.5 26.8 %collective-permute-start.24 = (bf16[384,512]{1,0:T(8,128)(2,1)S(1)}, bf16[384,512]{1,0:T(8,128)(2,1)S(1)}, u32[]{:S(2)}, u32[]{:S(2)}) collective-permute-start(bf16[384,512]{1,0:T(8,128)(2,1)S(1)} %copy-done.18), channel_id=1, source_target_pairs={{0,1},{1,2},{2,3},{4,5},{5,6},{6,7},{8,9},{9,10},{10,11},{12,13},{... | collective-permute-start | bytes 1179656 | tf_op jit(solution)/shard_map/ppermute | solution.py:401
  169.4 15.1 %collective-permute-start.25 = (bf16[384,512]{1,0:T(8,128)(2,1)S(1)}, bf16[384,512]{1,0:T(8,128)(2,1)S(1)}, u32[]{:S(2)}, u32[]{:S(2)}) collective-permute-start(bf16[384,512]{1,0:T(8,128)(2,1)S(1)} %copy-done.18), channel_id=1, source_target_pairs={{1,0},{2,1},{3,2},{5,4},{6,5},{7,6},{9,8},{10,9},{11,10},{13,12},{... | collective-permute-start | bytes 1179656 | tf_op jit(solution)/shard_map/ppermute | solution.py:402
  175.7 25.0 %collective-permute-start.26 = (bf16[384,512]{1,0:T(8,128)(2,1)S(1)}, bf16[384,512]{1,0:T(8,128)(2,1)S(1)}, u32[]{:S(2)}, u32[]{:S(2)}) collective-permute-start(bf16[384,512]{1,0:T(8,128)(2,1)S(1)} %copy-done.18), channel_id=1, source_target_pairs={{0,2},{1,3},{2,0},{3,1},{4,6},{5,7},{6,4},{7,5},{8,10},{9,11},{10,... | collective-permute-start | bytes 1179656 | tf_op jit(solution)/shard_map/ppermute | solution.py:400
  177.3 32.5 %collective-permute-start.19 = (bf16[384,512]{1,0:T(8,128)(2,1)}, bf16[384,512]{1,0:T(8,128)(2,1)S(1)}, u32[]{:S(2)}, u32[]{:S(2)}) collective-permute-start(bf16[384,512]{1,0:T(8,128)(2,1)} %collective-permute-done.18.far), channel_id=1, source_target_pairs={{2,3},{1,0},{6,7},{5,4},{10,11},{9,8},{14,15},{13,12},{18,19},{17,... | collective-permute-start | bytes 1179656 | tf_op jit(solution)/shard_map/ppermute | solution.py:403
  184.5 33.7 %collective-permute-start.23 = (bf16[384,512]{1,0:T(8,128)(2,1)S(1)}, bf16[384,512]{1,0:T(8,128)(2,1)S(1)}, u32[]{:S(2)}, u32[]{:S(2)}) collective-permute-start(bf16[384,512]{1,0:T(8,128)(2,1)S(1)} %collective-permute-done.22.far), channel_id=1, source_target_pairs={{2,3},{1,0},{6,7},{5,4},{10,11},{9,8},{14,15},{13,12},{18,19},{17,... | collective-permute-start | bytes 1179656 | tf_op jit(solution)/shard_map/ppermute | solution.py:403
  200.6 26.0 %collective-permute-start.27 = (bf16[384,512]{1,0:T(8,128)(2,1)S(1)}, bf16[384,512]{1,0:T(8,128)(2,1)S(1)}, u32[]{:S(2)}, u32[]{:S(2)}) collective-permute-start(bf16[384,512]{1,0:T(8,128)(2,1)S(1)} %collective-permute-done.26.far), channel_id=1, source_target_pairs={{2,3},{1,0},{6,7},{5,4},{10,11},{9,8},{14,15},{13,12},{18,19},{17,... | collective-permute-start | bytes 1179656 | tf_op jit(solution)/shard_map/ppermute | solution.py:403
  209.8 53.5 %collective-permute-start = (bf16[384,512]{1,0:T(8,128)(2,1)}, bf16[384,512]{1,0:T(8,128)(2,1)}, u32[]{:S(2)}, u32[]{:S(2)}) collective-permute-start(bf16[384,512]{1,0:T(8,128)(2,1)} %get-tuple-element.24), channel_id=1, source_target_pairs={{0,1},{1,2},{2,3},{4,5},{5,6},{6,7},{8,9},{9,10},{10,11},{12,13},{... | collective-permute-start | bytes 1179656 | tf_op jit(solution)/shard_map/ppermute | solution.py:401
  218.2 45.1 %collective-permute-start.1 = (bf16[384,512]{1,0:T(8,128)(2,1)}, bf16[384,512]{1,0:T(8,128)(2,1)}, u32[]{:S(2)}, u32[]{:S(2)}) collective-permute-start(bf16[384,512]{1,0:T(8,128)(2,1)} %get-tuple-element.24), channel_id=1, source_target_pairs={{1,0},{2,1},{3,2},{5,4},{6,5},{7,6},{9,8},{10,9},{11,10},{13,12},{... | collective-permute-start | bytes 1179656 | tf_op jit(solution)/shard_map/ppermute | solution.py:402
  227.4 35.9 %collective-permute-start.3 = (bf16[384,512]{1,0:T(8,128)(2,1)S(1)}, bf16[384,512]{1,0:T(8,128)(2,1)}, u32[]{:S(2)}, u32[]{:S(2)}) collective-permute-start(bf16[384,512]{1,0:T(8,128)(2,1)S(1)} %collective-permute-done.2.far), channel_id=1, source_target_pairs={{2,3},{1,0},{6,7},{5,4},{10,11},{9,8},{14,15},{13,12},{18,19},{17,... | collective-permute-start | bytes 1179656 | tf_op jit(solution)/shard_map/ppermute | solution.py:403
  (40 other events, 659.9 us)
